TPU v7x, 512 devices: a whole 4x4x16 slice. The times are simulated.
512 devices in a mesh: dp: 32 (over z_lo, x), mp: 16 (over z_hi, y, core).
Axes of the slice: x: 4, y: 4, z: 16 (z_hi: 2, z_lo: 8; z = z_hi * 8 + z_lo), core: 2. Of those that a mesh axis runs over, the one named last changes fastest.
Arguments:
- x_tiles: bfloat16 [32768, 6144], P('dp', 'mp')
- counts: int32 [32, 32], replicated, may hold values from 4 to 28, as said below
- owners: int32 [32, 32], replicated, may hold values from 0 to 31, as said below
- ln_gain: bfloat16 [6144], P('mp'), may hold values from 0.5 to 1.5
- w_up: bfloat16 [6144, 12288], P('dp', 'mp'), may hold values from -0.078125 to 0.078125
- up_bias: bfloat16 [12288], P('mp'), may hold values from -3 to 3
Outputs:
- hidden_act: bfloat16 [16384, 12288], P('dp', 'mp')
Inputs may be any that keep to these rules, and one draw needn't show every extreme that they name: Each row of owners is a permutation of 0 .. 31. Tile t of group s holds counts[s, t] patches in its first slots; every group takes exactly 512 patches in all.
All inputs are finite; a program needn't handle non-finite values.
Results may differ from a plain program's by a relative error of at most 0.0047.
Values may be sent and summed in bfloat16 or wider, within the bound.
No kernel may reach another device: no remote copies, remote signals or barrier semaphores. Data moves between devices by JAX's collectives and lax.ppermute only.
A program may use at most 64 MiB of HBM per device.

v0:
```python
import jax
import jax.numpy as jnp
from jax import lax
from jax.sharding import PartitionSpec as P

D = 6144
RECV = 512


def local(x_tiles, counts, owners, ln_gain, w_up, up_bias):
    groups = lax.axis_size("dp")
    my_index = lax.axis_index("dp")
    tile_rows = x_tiles.shape[0] // groups
    width_part = x_tiles.shape[1]
    tile_block = x_tiles.reshape(groups, tile_rows, width_part)
    inverse = jnp.argsort(owners, axis=1)
    my_tiles = lax.dynamic_index_in_dim(inverse, my_index, 0, keepdims=False)
    outgoing = jnp.take(tile_block, my_tiles, axis=0)
    incoming = lax.all_to_all(outgoing, "dp", split_axis=0, concat_axis=0, tiled=True)
    slot_count = incoming.shape[1]
    source_tiles = lax.dynamic_index_in_dim(inverse, my_index, 1, keepdims=False)
    held_rows = jnp.take_along_axis(counts, source_tiles[:, None], axis=1)[:, 0]
    inclusive = jnp.cumsum(held_rows)
    exclusive = inclusive - held_rows
    positions = jnp.arange(RECV, dtype=jnp.int32)
    source = jnp.sum((inclusive[None, :] <= positions[:, None]).astype(jnp.int32), axis=1)
    slot_index = positions - jnp.take(exclusive, source)
    flat_index = source * slot_count + slot_index
    packed = jnp.take(incoming.reshape(groups * slot_count, width_part), flat_index, axis=0)
    as_float = packed.astype(jnp.float32)
    row_sum, row_square = lax.psum(
        (jnp.sum(as_float, axis=1), jnp.sum(as_float * as_float, axis=1)), "mp"
    )
    row_mean = row_sum / D
    variance = row_square / D - row_mean * row_mean
    scaled = (
        (as_float - row_mean[:, None])
        * lax.rsqrt(variance + 1e-06)[:, None]
        * ln_gain.astype(jnp.float32)
    )
    normed = lax.all_gather(scaled.astype(jnp.bfloat16), "mp", axis=1, tiled=True)
    projected = jnp.dot(
        normed, lax.all_gather(w_up, "dp", axis=0, tiled=True), preferred_element_type=jnp.float32
    )
    return jax.nn.gelu(projected + up_bias.astype(jnp.float32), approximate=False).astype(
        jnp.bfloat16
    )


def solution(mesh):
    return jax.shard_map(
        local,
        mesh=mesh,
        in_specs=(P("dp", "mp"), P(), P(), P("mp"), P("dp", "mp"), P("mp")),
        out_specs=P("dp", "mp"),
        check_vma=False,
    )
```

profile of v0, /device:TPU:2, one launch (start us, length us, event | category | flops | bytes accessed | tf_op | source)
XLA Modules:
  0.0 536.9 jit_solution(3228038346032233318)
XLA Ops:
  6.5 0.9 copy.10
  7.4 0.8 sort.17
  8.2 0.2 dynamic-slice_reduce_fusion
  8.5 0.7 gather_fusion
  9.2 1.0 broadcast_select_fusion
  10.3 15.7 %all-to-all-start = ((bf16[32,32,384]{2,1,0:T(8,128)(2,1)}), bf16[32,32,384]{2,1,0:T(8,128)(2,1)S(1)}, u32[]{:S(2)}, u32[]{:S(2)}) async-start(bf16[32,32,384]{2,1,0:T(8,128)(2,1)} %broadcast_select_fusion), calls=%async_computation | async-start | bytes 1572864 | tf_op jit(solution)/shard_map/all_to_all | solution.py:19
  26.0 0.7 gather_fusion.2
  26.8 0.1 copy.11
  26.9 0.1 reduce
  27.0 0.7 fusion.18
  27.8 0.7 fusion.17
  28.5 0.1 convert_reduce_fusion.1
  28.6 4.4 compare_select_fusion.2
  33.0 0.2 compare_reduce_fusion.24
  33.1 15.7 %compare_and_fusion.1 = (pred[512]{0:T(512)(128)(4,1)S(1)}, s32[512]{0:T(512)S(1)}) fusion(s32[512]{0:T(512)S(1)} %convert_reduce_fusion.1, pred[512]{0:T(512)(128)(4,1)S(1)} %get-tuple-element.33, pred[512]{0:T(512)(128)(4,1)S(1)} %get-tuple-element.31, pred[512]{0:T(512)(128)(4,1)S(1)} %get-tuple-element.32, pred[512]{0:T(512)(128)(4,1)S(1)} %get-tuple-element.30, ...), kind=kLoop, calls=%fused_computation.79 | loop fusion | flops 20992 | bytes 19556 | tf_op jit(solution)/shard_map/jit(_take)/and | solution.py:29
  48.8 16.4 %all-to-all-done = bf16[32,32,384]{2,1,0:T(8,128)(2,1)S(1)} async-done(((bf16[32,32,384]{2,1,0:T(8,128)(2,1)}), bf16[32,32,384]{2,1,0:T(8,128)(2,1)S(1)}, u32[]{:S(2)}, u32[]{:S(2)}) %all-to-all-start) | async-done | bytes 786464 | tf_op jit(solution)/shard_map/all_to_all | solution.py:19
  65.3 1.9 gather_fusion.1
  67.2 0.4 convert_reduce_fusion
  67.6 67.1 %all-reduce = (f32[512]{0:T(512)S(1)}, f32[512]{0:T(512)S(1)}) all-reduce(f32[512]{0:T(512)S(1)} %get-tuple-element.8, f32[512]{0:T(512)S(1)} %get-tuple-element.7), channel_id=1, replica_groups=mesh['dp'=32,'mp'=16] {'mp'}, use_global_device_ids=true, to_apply=%region_6.7 | all-reduce | flops 1024 | bytes 8192 | tf_op jit(solution)/shard_map/psum | solution.py:31
  134.7 1.0 fusion.12
  135.8 0.7 all-gather.5.cloned.1.call-update
  136.5 140.3 %all-gather.3.cloned.1.call-done = bf16[512,6144]{1,0:T(8,128)(2,1)} async-done(((bf16[512,384]{1,0:T(8,128)(2,1)}), bf16[512,6144]{1,0:T(8,128)(2,1)}) %all-gather.3.cloned.1.call-update) | async-done | bytes 6291472 | tf_op jit(solution)/shard_map/all_gather | solution.py:41
  276.8 239.5 %all-gather.5.cloned.1.call-done = bf16[6144,768]{1,0:T(8,128)(2,1)} async-done(((bf16[192,768]{1,0:T(8,128)(2,1)}), bf16[6144,768]{1,0:T(8,128)(2,1)}) %all-gather.5.cloned.1.call-update) | async-done | bytes 9437200 | tf_op jit(solution)/shard_map/all_gather | solution.py:43
  516.4 13.7 %fusion.2 = bf16[512,768]{1,0:T(8,128)(2,1)} fusion(bf16[512,6144]{1,0:T(8,128)(2,1)} %all-gather.3.cloned.1.call-done, bf16[6144,768]{1,0:T(8,128)(2,1)} %all-gather.5.cloned.1.call-done, f32[768]{0:T(1024)S(1)} %convert_element_type.22), kind=kOutput, calls=%fused_computation.6 | convolution fusion | flops 4857790464 | bytes 16518144 | tf_op jit(solution)/shard_map/dot_general | solution.py:42
  (26 shorter events, 0.3 us)
Async XLA Ops:
  6.5 1.9 copy-start
  9.2 16.8 %copy-start.3 = (bf16[384]{0:T(512)(128)(2,1)S(1)}, bf16[384]{0:T(512)(128)(2,1)}, u32[]{:S(2)}) copy-start(bf16[384]{0:T(512)(128)(2,1)} %param.9) | copy-start | bytes 2308
  9.2 16.8 %copy-start.1 = (s32[32,32]{1,0:T(8,128)S(1)}, s32[32,32]{1,0:T(8,128)}, u32[]{:S(2)}) copy-start(s32[32,32]{1,0:T(8,128)} %param.7) | copy-start | bytes 12292
  10.3 55.0 %all-to-all-start = ((bf16[32,32,384]{2,1,0:T(8,128)(2,1)}), bf16[32,32,384]{2,1,0:T(8,128)(2,1)S(1)}, u32[]{:S(2)}, u32[]{:S(2)}) async-start(bf16[32,32,384]{2,1,0:T(8,128)(2,1)} %broadcast_select_fusion), calls=%async_computation | async-start | bytes 1572864 | tf_op jit(solution)/shard_map/all_to_all | solution.py:19
  26.0 250.9 %all-gather.3.cloned.1.call-start = ((), (), s32[]{:S(2)}) async-start(), calls=%async_computation.1 | async-start | bytes 6684672 | tf_op jit(solution)/shard_map/all_gather | solution.py:41
  67.2 69.3 %copy-start.2 = (bf16[768]{0:T(1024)(128)(2,1)S(1)}, bf16[768]{0:T(1024)(128)(2,1)}, u32[]{:S(2)}) copy-start(bf16[768]{0:T(1024)(128)(2,1)} %param.11) | copy-start | bytes 4612
  135.8 380.6 %all-gather.5.cloned.1.call-start = ((), (), s32[]{:S(2)}) async-start(), calls=%async_computation.2 | async-start | bytes 9732096 | tf_op jit(solution)/shard_map/all_gather | solution.py:43
Sparse Core Ops, SparseCore 0:
  135.9 140.8 all-gather.2
  278.9 237.4 all-gather.4
where the time goes:
time: 537 us
  waiting for transfers between devices  397 us (74%)
  blocking collectives  67.1 us (12%)
  other arithmetic  23.8 us (4%)
  starting transfers between devices  15.8 us (3%)
  matrix products  13.7 us (3%)
  between operations  13.6 us (3%)
  local copies, waits for them, and re-layouts  5.97 us (1%)
    all_gather x1, waiting for transfers between devices, local(): lax.all_gather(w_up, 'dp', axis=0, tiled=True)  240 us
    all_gather x1, waiting for transfers between devices, local(): lax.all_gather(scaled.astype(jnp.bfloat16), 'mp', axis=1, tiled=True)  140 us
    psum x1, blocking collectives, local(): lax.psum((jnp.sum(as_float, axis=1), jnp.sum(as_float * as_float, axis=1)...  67.1 us
    all_to_all x1, waiting for transfers between devices, local(): lax.all_to_all(outgoing, 'dp', split_axis=0, concat_axis=0, tiled=True)  16.4 us
    and x1, other arithmetic, local(): jnp.take(incoming.reshape(groups * slot_count, width_part), flat_index, a...  15.7 us
    all_to_all x1, starting transfers between devices, local(): lax.all_to_all(outgoing, 'dp', split_axis=0, concat_axis=0, tiled=True)  15.7 us
    dot_general x1, matrix products, local(): jnp.dot(normed, lax.all_gather(w_up, 'dp', axis=0, tiled=True), preferred...  13.7 us
  transfers between devices with their start and end apart: 3, of which 3 were waited for; matrix products, arithmetic and copies ran while one was open for 4% of the time, Pallas kernels for 0%

commit v1 on v0

--- a/solution.py
+++ b/solution.py
@@ -38,7 +38,10 @@
         * lax.rsqrt(variance + 1e-06)[:, None]
         * ln_gain.astype(jnp.float32)
     )
-    normed = lax.all_gather(scaled.astype(jnp.bfloat16), "mp", axis=1, tiled=True)
+    normed = jnp.concatenate(
+        lax.all_to_all(jnp.stack([scaled.astype(jnp.bfloat16)] * lax.axis_size("mp")), "mp", 0, 0),
+        axis=1,
+    )
     projected = jnp.dot(
         normed, lax.all_gather(w_up, "dp", axis=0, tiled=True), preferred_element_type=jnp.float32
     )

time: 537 us -> 624 us (1.16)
  the two profiles are of different devices: /device:TPU:2 before, /device:TPU:264 now
where the time goes in v1:
time: 624 us; the launch traced here: 623 us
  waiting for transfers between devices  478 us (77%)
  blocking collectives  52.2 us (8%)
  starting transfers between devices  32.6 us (5%)
  other arithmetic  23.1 us (4%)
  matrix products  13.8 us (2%)
  between operations  13.6 us (2%)
  local copies, waits for them, and re-layouts  9.39 us (2%)
    all_gather x1, waiting for transfers between devices, local(): lax.all_gather(w_up, 'dp', axis=0, tiled=True)  460 us
    psum x1, blocking collectives, local(): lax.psum((jnp.sum(as_float, axis=1), jnp.sum(as_float * as_float, axis=1)...  52.2 us
    all_to_all x1, starting transfers between devices, local(): lax.all_to_all(jnp.stack([scaled.astype(jnp.bfloat16)] * lax.axis_size('m...  24.7 us
    all_to_all x1, waiting for transfers between devices, local(): lax.all_to_all(outgoing, 'dp', split_axis=0, concat_axis=0, tiled=True)  18.1 us
    and x1, other arithmetic, local(): jnp.take(incoming.reshape(groups * slot_count, width_part), flat_index, a...  15.7 us
    dot_general x1, matrix products, local(): jnp.dot(normed, lax.all_gather(w_up, 'dp', axis=0, tiled=True), preferred...  13.8 us
  transfers between devices with their start and end apart: 3, of which 2 were waited for; matrix products, arithmetic and copies ran while one was open for 4% of the time, Pallas kernels for 0%

profile of v1, /device:TPU:264, one launch (start us, length us, event | category | flops | bytes accessed | tf_op | source)
XLA Modules:
  0.0 623.1 jit_solution(15422080609335362725)
XLA Ops:
  6.5 0.9 copy.11
  7.4 0.8 sort.17
  8.2 0.2 dynamic-slice_reduce_fusion
  8.5 0.7 gather_fusion
  9.2 1.0 broadcast_select_fusion
  10.3 7.9 %all-to-all-start = ((bf16[32,32,384]{2,1,0:T(8,128)(2,1)}), bf16[32,32,384]{2,1,0:T(8,128)(2,1)S(1)}, u32[]{:S(2)}, u32[]{:S(2)}) async-start(bf16[32,32,384]{2,1,0:T(8,128)(2,1)} %broadcast_select_fusion), calls=%async_computation | async-start | bytes 1572864 | tf_op jit(solution)/shard_map/all_to_all | solution.py:19
  18.2 0.7 gather_fusion.2
  19.0 0.1 reduce
  19.2 0.7 fusion.18
  19.9 0.7 fusion.17
  20.7 4.4 compare_select_fusion.2
  25.1 0.2 compare_reduce_fusion.24
  25.3 15.7 %compare_and_fusion.1 = (pred[512]{0:T(512)(128)(4,1)S(1)}, s32[512]{0:T(512)S(1)}) fusion(s32[512]{0:T(512)S(1)} %convert_reduce_fusion.1, pred[512]{0:T(512)(128)(4,1)S(1)} %get-tuple-element.33, pred[512]{0:T(512)(128)(4,1)S(1)} %get-tuple-element.31, pred[512]{0:T(512)(128)(4,1)S(1)} %get-tuple-element.32, pred[512]{0:T(512)(128)(4,1)S(1)} %get-tuple-element.30, ...), kind=kLoop, calls=%fused_computation.79 | loop fusion | flops 20992 | bytes 19556 | tf_op jit(solution)/shard_map/jit(_take)/and | solution.py:29
  41.0 18.1 %all-to-all-done = bf16[32,32,384]{2,1,0:T(8,128)(2,1)S(1)} async-done(((bf16[32,32,384]{2,1,0:T(8,128)(2,1)}), bf16[32,32,384]{2,1,0:T(8,128)(2,1)S(1)}, u32[]{:S(2)}, u32[]{:S(2)}) %all-to-all-start) | async-done | bytes 786464 | tf_op jit(solution)/shard_map/all_to_all | solution.py:19
  59.1 1.9 gather_fusion.1
  61.0 0.4 convert_reduce_fusion
  61.4 52.2 %all-reduce = (f32[512]{0:T(512)S(1)}, f32[512]{0:T(512)S(1)}) all-reduce(f32[512]{0:T(512)S(1)} %get-tuple-element.8, f32[512]{0:T(512)S(1)} %get-tuple-element.7), channel_id=1, replica_groups=mesh['dp'=32,'mp'=16] {'mp'}, use_global_device_ids=true, to_apply=%region_6.7 | all-reduce | flops 1024 | bytes 8192 | tf_op jit(solution)/shard_map/psum | solution.py:31
  113.7 0.3 fusion.12
  114.0 0.2 copy.13
  114.2 3.2 stack.2
  117.4 24.7 %all-to-all-start.1 = ((bf16[16,512,384]{1,2,0:T(8,128)(2,1)}), bf16[16,512,384]{1,2,0:T(8,128)(2,1)}, u32[]{:S(2)}, u32[]{:S(2)}) async-start(bf16[16,512,384]{1,2,0:T(8,128)(2,1)} %stack.2), calls=%async_computation.1 | async-start | bytes 12582912 | tf_op jit(solution)/shard_map/all_to_all | solution.py:42
  142.1 0.7 all-gather.2.cloned.1.call-update
  142.8 459.7 %all-gather.2.cloned.1.call-done = bf16[6144,768]{1,0:T(8,128)(2,1)} async-done(((bf16[192,768]{1,0:T(8,128)(2,1)}), bf16[6144,768]{1,0:T(8,128)(2,1)}) %all-gather.2.cloned.1.call-update) | async-done | bytes 9437200 | tf_op jit(solution)/shard_map/all_gather | solution.py:46
  602.5 13.8 %fusion.2 = bf16[512,768]{1,0:T(8,128)(2,1)} fusion(bf16[512,6144]{0,1:T(8,128)(2,1)} %bitcast.45, bf16[6144,768]{1,0:T(8,128)(2,1)} %all-gather.2.cloned.1.call-done, f32[768]{0:T(1024)S(1)} %convert_element_type.26), kind=kOutput, calls=%fused_computation.6 | convolution fusion | flops 4857790464 | bytes 16518144 | tf_op jit(solution)/shard_map/dot_general | solution.py:45
  (27 shorter events, 0.4 us)
Async XLA Ops:
  6.5 1.9 copy-start
  9.2 8.9 %copy-start.1 = (s32[32,32]{1,0:T(8,128)S(1)}, s32[32,32]{1,0:T(8,128)}, u32[]{:S(2)}) copy-start(s32[32,32]{1,0:T(8,128)} %param.7) | copy-start | bytes 12292
  9.2 9.9 %copy-start.3 = (bf16[384]{0:T(512)(128)(2,1)S(1)}, bf16[384]{0:T(512)(128)(2,1)}, u32[]{:S(2)}) copy-start(bf16[384]{0:T(512)(128)(2,1)} %param.9) | copy-start | bytes 2308
  10.3 48.8 %all-to-all-start = ((bf16[32,32,384]{2,1,0:T(8,128)(2,1)}), bf16[32,32,384]{2,1,0:T(8,128)(2,1)S(1)}, u32[]{:S(2)}, u32[]{:S(2)}) async-start(bf16[32,32,384]{2,1,0:T(8,128)(2,1)} %broadcast_select_fusion), calls=%async_computation | async-start | bytes 1572864 | tf_op jit(solution)/shard_map/all_to_all | solution.py:19
  117.4 25.4 %copy-start.2 = (bf16[768]{0:T(1024)(128)(2,1)S(1)}, bf16[768]{0:T(1024)(128)(2,1)}, u32[]{:S(2)}) copy-start(bf16[768]{0:T(1024)(128)(2,1)} %param.11) | copy-start | bytes 4612
  117.4 485.1 %all-to-all-start.1 = ((bf16[16,512,384]{1,2,0:T(8,128)(2,1)}), bf16[16,512,384]{1,2,0:T(8,128)(2,1)}, u32[]{:S(2)}, u32[]{:S(2)}) async-start(bf16[16,512,384]{1,2,0:T(8,128)(2,1)} %stack.2), calls=%async_computation.1 | async-start | bytes 12582912 | tf_op jit(solution)/shard_map/all_to_all | solution.py:42
  142.1 460.4 %all-gather.2.cloned.1.call-start = ((), (), s32[]{:S(2)}) async-start(), calls=%async_computation.2 | async-start | bytes 9732096 | tf_op jit(solution)/shard_map/all_gather | solution.py:46
Sparse Core Ops, SparseCore 0:
  145.0 457.4 all-gather.1
